TPU v7x, 512 devices: a whole 4x4x16 slice. The times are simulated.
512 devices in a mesh: group: 8 (over y, core), box: 64 (over z, x).
Axes of the slice: x: 4, y: 4, z: 16, core: 2. Of those that a mesh axis runs over, the one named last changes fastest.
Arguments:
- dipoles: float32 [3, 131072], P(None, ('group', 'box')), may hold values from -6 to 6
- perm_field: float32 [3, 131072], P(None, ('group', 'box')), may hold values from -6 to 6
- positions: float32 [3, 131072], P(None, ('group', 'box')), may hold values from -1 to 1
- polarizability: float32 [131072], P(('group', 'box')), may hold values from 0.5 to 2.5
- occupancy: int32 [1024], P(('group', 'box')), may hold values from 1 to 128
- far_boxes: int32 [1024, 189], P(('group', 'box')), may hold values from 0 to 1023, as said below
- far_class: int32 [1024, 189], P(('group', 'box')), may hold values from 0 to 7
- far_count: int32 [1024], P(('group', 'box')), may hold values from 94 to 189
- far_scale: float32 [1024, 189], P(('group', 'box')), may hold values from 0.2 to 1
- translations: float32 [8, 165, 165], replicated, may hold values from -0.0015015624 to 0.0015015624
Outputs:
- new_dipoles: float32 [3, 131072], P(None, ('group', 'box'))
- residual: float32 [3, 131072], P(None, ('group', 'box'))
Inputs may be any that keep to these rules, and one draw needn't show every extreme that they name: Entry far_boxes[b, e] names a box of layer z' in group g' with |z' - z| <= 4 for box b's own layer z and group g, and |z' - z| >= 2 where g' = g; the first entry of every list is 4 layers away.
All inputs are finite; a program needn't handle non-finite values.
Results may differ from a plain program's by a relative error of at most 0.0003.
Values sent between devices are 32-bit elements; how exact they have to be, the bound alone decides.
No kernel may reach another device: no remote copies, remote signals or barrier semaphores. Data moves between devices by JAX's collectives and lax.ppermute only.
A program may use at most 64 MiB of HBM per device.

v0:
```python
import jax
import jax.numpy as jnp
from jax import lax
from jax.experimental import pallas as pl
from jax.experimental.pallas import tpu as pltpu
from jax.sharding import Mesh
from jax.sharding import PartitionSpec as P

TILE = 128
ORDER = 8
NTERM = 165
REST = NTERM - TILE
ILIST = 189
CLASSES = 8
GROUPS = 8
OWNERS = 64
NX = 4
NY = 4
PLANE = NX * NY
CHUNK = 40
F32 = jnp.float32
BF16 = jnp.bfloat16

HALF = 5.4
ROOT_THOLE = 0.39**0.5
NT = (((1,), (1,)), ((), ()))
NN = (((1,), (0,)), ((), ()))


def term_table():
    listing = []
    for degree in range(ORDER + 1):
        for first in range(degree + 1):
            for second in range(degree + 1 - first):
                listing.append((first, second, degree - first - second))
    return listing


TERMS = term_table()


def dot(a, b, dims):
    return lax.dot_general(a, b, dims, preferred_element_type=F32)


def halves(x):
    high = x.astype(BF16)
    return high, (x - high.astype(F32)).astype(BF16)


def dot_three(a, b, dims):
    a_high, a_low = halves(a)
    b_high, b_low = halves(b)
    return dot(a_high, b_high, dims) + (dot(a_high, b_low, dims) + dot(a_low, b_high, dims))


def chebyshev(coord):
    series = [None, coord]
    doubled = 2.0 * coord
    series.append(doubled * coord - 1.0)
    for _ in range(3, ORDER + 1):
        series.append(doubled * series[-1] - series[-2])
    return series


def write_monomials(ref, px, py, pz):
    cx, cy, cz = chebyshev(px), chebyshev(py), chebyshev(pz)
    cross = {}
    for t, (i, j, k) in enumerate(TERMS):
        if (i, j) not in cross:
            if i and j:
                cross[i, j] = cx[i] * cy[j]
            else:
                cross[i, j] = cx[i] if i else cy[j]
        head = cross[i, j]
        if head is None:
            value = jnp.ones_like(px) if k == 0 else cz[k]
        else:
            value = head if k == 0 else head * cz[k]
        ref[t * 8 : t * 8 + 8, :] = value


def own_place():
    me = lax.axis_index("d")
    return (me // OWNERS) & 1, (me // NX) & (OWNERS // NX - 1), me & (NX - 1), (me // (2 * OWNERS)) * NX


def first_kernel(
    occ_hbm, count_hbm, dip_hbm, perm_hbm, pos_hbm, pol_hbm, boxes_hbm, class_hbm, scale_hbm, out_ref,
    mono, chunk, dip_ref, perm_ref, pos_ref, pol_ref, scale_ref, boxes_ref, class_ref, occ_ref, count_ref, sems,
):
    pairs = (
        (pos_hbm, pos_ref), (dip_hbm, dip_ref), (pol_hbm, pol_ref), (perm_hbm, perm_ref),
        (boxes_hbm, boxes_ref), (class_hbm, class_ref), (scale_hbm, scale_ref), (occ_hbm, occ_ref), (count_hbm, count_ref),
    )
    copies = [pltpu.make_async_copy(source, target, sems.at[n]) for n, (source, target) in enumerate(pairs)]
    for copy in copies:
        copy.start()
    chunk[...] = jnp.zeros_like(chunk)
    lane = lax.broadcasted_iota(jnp.int32, (1, TILE), 1)
    for copy in copies:
        copy.wait()
    for w in range(2):
        live = (lane < occ_ref[w]).astype(F32)
        lanes = slice(w * TILE, (w + 1) * TILE)
        base = 8 + w * 8
        chunk[base : base + 3, :] = pos_ref[:, lanes]
        chunk[base + 3 : base + 4, :] = pol_ref[:, lanes]
        chunk[base + 4 : base + 7, :] = dip_ref[:, lanes] * live
        chunk[base + 7 : base + 8, :] = live
        chunk[24 + w * 3 : 27 + w * 3, :] = perm_ref[:, lanes]
    plane = own_place()[1]
    box = boxes_ref[...]
    within = box & 1
    layer = (box >> 1) & (OWNERS - 1)
    group = box >> 7
    step = (layer >> 2) - plane
    stack = jnp.where(step == 0, 0, jnp.where(step < 0, 1, 2))
    place = within * 96 + stack * 32 + (group & 1) * PLANE + (group >> 1) * NX + (layer & 3)
    place = place.astype(F32)
    kind = class_ref[...].astype(F32)
    entry = lax.broadcasted_iota(jnp.int32, (1, ILIST), 1)
    for w in range(2):
        weight = scale_ref[w : w + 1, :] * (entry < count_ref[w]).astype(F32)
        for n, row in enumerate((place[w : w + 1, :], kind[w : w + 1, :], weight)):
            chunk[30 + w * 3 + n : 31 + w * 3 + n, :] = row[:, :TILE]
            chunk[36 + n : 37 + n, w * 64 : w * 64 + ILIST - TILE] = row[:, TILE:]
    def both(row):
        two = chunk[pl.ds(8 + row, 2, stride=8), :]
        return jnp.concatenate([two, two, two, two], axis=0)

    write_monomials(mono, both(0), both(1), both(2))
    for w in range(2):
        terms = mono[pl.ds(w, NTERM, stride=8), :]
        moment = dot_three(chunk[12 + w * 8 : 15 + w * 8, :], terms, NT)
        for c in range(3):
            chunk[c * 2 + w : c * 2 + w + 1, :] = moment[c : c + 1, :TILE]
            chunk[6 + w : 7 + w, c * REST : (c + 1) * REST] = moment[c : c + 1, TILE:]
    whole = chunk[...]
    for m in range(PLANE):
        out_ref[m, :, :] = whole


def write_fields(rows_ref, number, px, py, pz, root, first_layer):
    box = lax.broadcasted_iota(jnp.int32, (number, TILE), 0)
    rows_ref[pl.ds(0, number, stride=8), :] = HALF * (px + 2.0 * (box & 1).astype(F32))
    rows_ref[pl.ds(1, number, stride=8), :] = HALF * py
    rows_ref[pl.ds(2, number, stride=8), :] = HALF * (pz + 2.0 * ((box >> 1) + first_layer).astype(F32))
    rows_ref[pl.ds(3, number, stride=8), :] = root


def root_of(pol):
    return jnp.where(pol > 0.0, ROOT_THOLE * lax.rsqrt(jnp.where(pol > 0.0, pol, 1.0)), 0.0)


def scalars(delta, roots):
    dx, dy, dz = delta
    squared = dx * dx + dy * dy + (dz * dz + 1.0)
    inverse = lax.rsqrt(squared)
    inv_two = inverse * inverse
    inv_three = inverse * inv_two
    minus = (squared * (squared * inverse)) * roots
    damping = jnp.exp(minus)
    lambda_three = 1.0 - damping
    lambda_five = lambda_three + minus * damping
    return (3.0 * lambda_five) * (inv_three * inv_two), lambda_three * inv_three


def field_of(delta, radial, direct, moment):
    along = radial * (delta[0] * moment[0] + delta[1] * moment[1] + delta[2] * moment[2])
    return [delta[c] * along - direct * moment[c] for c in range(3)]


def added(parts):
    while len(parts) > 1:
        parts = [parts[i] + parts[i + 1] if i + 1 < len(parts) else parts[i] for i in range(0, len(parts), 2)]
    return parts[0]


def row(ref, at):
    return ref[pl.ds(at, 8, stride=0), :]


def tile_at(n, base=0):
    return pl.ds(pl.multiple_of(base + n * 8, 8), 8)


def trips_of(live):
    count = jnp.sum(live, axis=1, keepdims=True)
    return ((count + 7.0) * 0.125).astype(jnp.int32)


def spread(wide_ref, cols, boxes, fields):
    for slot, box in enumerate(boxes):
        for f in fields:
            at = box * 8 + f
            value = jnp.broadcast_to(cols[:, at : at + 1], (TILE, TILE))
            wide_ref[f, slot * TILE : (slot + 1) * TILE, :] = -value if f == 3 else value


def near_boxes(total_ref, slots, wide_ref, targets, trips, rows_ref, sources, keep_ref, first_kept):
    half = keep_ref.shape[0] // 2

    def body(n, carry):
        mine = [[wide_ref[f, tile_at(n, target * TILE), :] for f in range(4)] for target in targets]
        parts = [[] for _ in targets]
        for k, box in enumerate(sources):
            where = [row(rows_ref, box * 8 + f) for f in range(7)]
            for i, spot in enumerate(mine):
                delta = [spot[c] - where[c] for c in range(3)]
                radial, direct = scalars(delta, spot[3] * where[3])
                kept = tile_at(n, slots[i] * TILE)
                keep_ref[first_kept + k, kept, :] = radial
                keep_ref[half + first_kept + k, kept, :] = direct
                parts[i].append(field_of(delta, radial, direct, where[4:7]))
        for i, slot in enumerate(slots):
            for c in range(3):
                total_ref[c, tile_at(n, slot * TILE), :] = added([part[c] for part in parts[i]])
        return carry

    lax.fori_loop(0, trips, body, 0)


def lane_sums(total_ref, c, slot):
    return jnp.sum(jnp.transpose(total_ref[c, slot * TILE : (slot + 1) * TILE, :]), axis=0, keepdims=True)


def self_term(root):
    return 1.0 - jnp.exp(-(root * root))


def prepare_kernel(trans_ref, high_ref, low_ref):
    high_ref[...] = jnp.zeros_like(high_ref)
    low_ref[...] = jnp.zeros_like(low_ref)
    for o in range(CLASSES):
        high, low = halves(jnp.transpose(trans_ref[:, o, :]))
        high_ref[o * 256 : o * 256 + NTERM, :] = high
        low_ref[o * 256 : o * 256 + NTERM, :] = low


def second_kernel(block_ref, sel_ref, near_ref, wide, m_high_ref, m_low_ref, keep, rows, total, mono):
    mine = own_place()[3]
    rows[...] = jnp.zeros_like(rows)
    for x in range(NX):
        rows[x * 16 : x * 16 + 16, :] = block_ref[mine + x, 8:24, :]

    def field(f):
        return rows[pl.ds(f, 8, stride=8), :]

    px, py, pz, root = field(0), field(1), field(2), root_of(field(3))
    trips = trips_of(field(7))
    write_monomials(mono, px, py, pz)
    write_fields(rows, 8, px, py, pz, root, 0)
    spread(wide, jnp.transpose(rows[...]), range(8), range(4))
    for k in range(8):
        high, low = halves(mono[pl.ds(k, NTERM, stride=8), :])
        m_high_ref[k * 176 : k * 176 + NTERM, :] = high
        m_low_ref[k * 176 : k * 176 + NTERM, :] = low
    for box in range(8):
        low, high = max(box // 2 - 1, 0), min(box // 2 + 1, NX - 1)
        sources = range(low * 2, high * 2 + 2)
        near_boxes(total, [box], wide, [box], trips[box, 0], rows, sources, keep, low * 2 - (box // 2 - 1) * 2)
    spot = lax.broadcasted_iota(jnp.int32, (192, TILE), 0)
    kinds = lax.broadcasted_iota(jnp.int32, (CLASSES, TILE), 0)
    side = lax.broadcasted_iota(jnp.int32, (CLASSES, TILE), 1) >> 6
    for x in range(NX):
        got = jnp.zeros((32, 192), F32)
        first, second = [], []
        for w in range(2):
            at = 30 + w * 3
            place = block_ref[mine + x, at : at + 1, :].astype(jnp.int32)
            kind = block_ref[mine + x, at + 1 : at + 2, :].astype(jnp.int32)
            weight = jnp.where(kinds == kind, block_ref[mine + x, at + 2 : at + 3, :], 0.0)
            chosen = jnp.where(spot == place, 1.0, 0.0).astype(BF16)
            high = weight.astype(BF16).astype(F32)
            first.append(dot(jnp.concatenate([high, weight - high], axis=0).astype(BF16), chosen, NT))
        place = block_ref[mine + x, 36:37, :].astype(jnp.int32)
        kind = block_ref[mine + x, 37:38, :].astype(jnp.int32)
        weight = jnp.where(kinds == kind, block_ref[mine + x, 38:39, :], 0.0)
        high = weight.astype(BF16).astype(F32)
        low = weight - high
        both = [jnp.where(side == w, part, 0.0) for w in range(2) for part in (high, low)]
        chosen = jnp.where(spot == place, 1.0, 0.0).astype(BF16)
        second = dot(jnp.concatenate(both, axis=0).astype(BF16), chosen, NT)
        for w in range(2):
            k = x * 2 + w
            tail = second[w * 16 : w * 16 + 16]
            sel_ref[k * 8 : k * 8 + 8, :] = (first[w][0:8] + tail[0:8]) + (first[w][8:16] + tail[8:16])
    for c in range(3):
        for box in range(8):
            near_ref[c * 8 + box : c * 8 + box + 1, :] = lane_sums(total, c, box)


def third_kernel(
    block_ref, own_ref, sides_ref, sel_ref, near_ref, wide_ref, m_high_ref, m_low_ref, t_high_ref, t_low_ref,
    res_ref, send_ref, keep, summed, head, rest, far, rows, total,
):
    core, _, x_me, mine = own_place()
    sel_high, sel_low = halves(sel_ref[...])
    both = jnp.concatenate([sel_high, sel_low], axis=0)
    for kind in range(4):
        pieces = []
        for w in range(2):
            pieces += [own_ref[pl.ds(at + kind * 2 + w, 16, stride=8), :] for at in (0, OWN_ROWS)]
            pieces += [sides_ref[pl.ds(at + kind * 2 + w, 32, stride=8), :] for at in (0, SIDE_ROWS)]
        high, low = halves(jnp.concatenate(pieces, axis=0))
        got = dot(both, high, NN)
        summed[kind * 64 : kind * 64 + 64, :] = got[0:64] + (got[64:128] + dot(sel_high, low, NN))
    parts = []
    for c in range(3):
        pieces = []
        for o in range(CLASSES):
            pieces.append(summed[pl.ds(c * 64 + o, 8, stride=8), :])
            tail = summed[pl.ds(192 + o, 8, stride=8), :][:, c * REST : (c + 1) * REST]
            pieces.append(jnp.concatenate([tail, jnp.zeros((8, TILE - REST), F32)], axis=1))
        parts.append(jnp.concatenate(pieces, axis=1))
    parts.append(jnp.zeros((8, CLASSES * 256), F32))
    high, low = halves(jnp.concatenate(parts, axis=0))
    got = dot(jnp.concatenate([high, low], axis=0), t_high_ref[...], NN)
    moved = got[0:24] + (got[32:56] + dot(high, t_low_ref[...], NN)[0:24])
    moved_high = moved.astype(BF16).astype(F32)
    for n, part in enumerate((moved_high, moved - moved_high)):
        head[n * 24 : n * 24 + 24, :] = part[:, 0:TILE]
        rest[n * 24 : n * 24 + 24, 0:REST] = part[:, TILE:]
    rows[...] = jnp.zeros_like(rows)
    rows[0:16, :] = sides_ref[pl.ds(pl.multiple_of(272 + 32 * core, 8), 16), :]
    for x in range(NX):
        rows[16 + x * 16 : 32 + x * 16, :] = block_ref[mine + x, 8:24, :]
    rows[80:96, :] = sides_ref[pl.ds(pl.multiple_of(SIDE_ROWS + 256 + 32 * core, 8), 16), :]

    def field(f):
        return rows[pl.ds(f, 12, stride=8), :]

    px, py, pz, pol = field(0), field(1), field(2), field(3)
    live = rows[pl.ds(16 + 7, 8, stride=8), :]
    source = [rows[pl.ds(16 + 4 + c, 8, stride=8), :] for c in range(3)]
    root = root_of(pol)
    trips = trips_of(live)
    write_fields(rows, 12, px, py, pz, root, -1)
    for slots, boxes, sources in (((0, 1), (0, 1), (0, 1)), ((2, 3), (6, 7), (10, 11))):
        most = jnp.maximum(trips[boxes[0], 0], trips[boxes[1], 0])
        near_boxes(total, slots, wide_ref, boxes, most, rows, sources, keep, 0)
    for k in range(8):
        left = jnp.concatenate([head[pl.ds(k, 6, stride=8), :], rest[pl.ds(k, 6, stride=8), :][:, 0:REST]], axis=1)
        left = left.astype(BF16)
        with_high = dot(left, m_high_ref[k * 176 : k * 176 + NTERM, :], NN)
        with_low = dot(left, m_low_ref[k * 176 : k * 176 + NTERM, :], NN)
        value = with_high[0:3] + (with_high[3:6] + with_low[0:3])
        for c in range(3):
            far[c * 8 + k : c * 8 + k + 1, :] = value[c : c + 1]
    alone = self_term(root[2:10])
    nothing = jnp.zeros((4, TILE), F32)
    for c in range(3):
        perm = jnp.concatenate(
            [block_ref[mine + x, 24 + w * 3 + c : 25 + w * 3 + c, :] for x in range(NX) for w in range(2)], axis=0
        )
        ends = [lane_sums(total, c, slot) for slot in range(4)]
        edge = jnp.concatenate(ends[0:2] + [nothing] + ends[2:4], axis=0)
        near_zero = near_ref[c * 8 : c * 8 + 8, :] + edge + alone * source[c]
        res_ref[c * 8 : c * 8 + 8, :] = jnp.where(
            live > 0.0, perm + far[c * 8 : c * 8 + 8, :] + near_zero - source[c] / pol[2:10], 0.0
        )
    first = jnp.where(x_me < 2, 4, 0)
    for c in range(3):
        for k in range(4):
            send_ref[c * 4 + k : c * 4 + k + 1, :] = res_ref[pl.ds(c * 8 + first + k, 1), :]


def window_kernel(block_ref, sides_ref, rows, keep, edge, every):
    core, _, x_me, mine = own_place()
    first = x_me * 2
    every[0:32, :] = sides_ref[pl.ds(pl.multiple_of(256 + 32 * core, 8), 32), :]
    for x in range(NX):
        every[32 + x * 16 : 48 + x * 16, :] = block_ref[mine + x, 8:24, :]
    every[96:128, :] = sides_ref[pl.ds(pl.multiple_of(SIDE_ROWS + 256 + 32 * core, 8), 32), :]
    rows[...] = jnp.zeros_like(rows)
    for k in range(10):
        rows[k * 8 : k * 8 + 8, :] = every[pl.ds(pl.multiple_of((first + k) * 8, 8), 8), :]

    def field(f):
        return rows[pl.ds(f, 10, stride=8), :]

    px, py, pz, pol, live = field(0), field(1), field(2), field(3), field(7)
    root = root_of(pol)
    rows[80:90, :] = pol
    rows[96:106, :] = self_term(root)
    trips = trips_of(live)
    write_fields(rows, 10, px, py, pz, root, x_me - 2)
    for outside, layer in ((x_me == 0, 1), (x_me == NX - 1, 3)):

        @pl.when(outside)
        def _():
            cols = jnp.transpose(rows[...])
            spread(edge, cols, (layer * 2, layer * 2 + 1), range(4))
            for w in range(2):

                def body(n, carry):
                    for u in range(2):
                        at = tile_at(n * 2 + u, w * TILE)
                        spot = [edge[f, at, :] for f in range(4)]
                        for k in range(6):
                            source = (layer - 1) * 2 + k
                            delta = [spot[c] - row(rows, source * 8 + c) for c in range(3)]
                            radial, direct = scalars(delta, spot[3] * row(rows, source * 8 + 3))
                            keep[k, at, :] = radial
                            keep[6 + k, at, :] = direct
                    return carry

                lax.fori_loop(0, (trips[layer * 2 + w, 0] + 1) // 2, body, 0)


def fourth_kernel(
    rows_ref, plane_keep, edge_keep, out_keep, plane_wide, out_wide, res_ref, got_ref, new_ref, out_ref,
    moved, rows, total, two_ref,
):
    x_me = own_place()[2]
    first = x_me * 2
    for c in range(3):
        got = got_ref[c * 4 : c * 4 + 4, :]
        moved[c, 0:4, :] = got
        moved[c, 4:12, :] = res_ref[c * 8 : c * 8 + 8, :]
        moved[c, 12:16, :] = got
    rows[...] = rows_ref[...]
    pol, alone = rows[80:90, :], rows[96:106, :]
    live = rows[pl.ds(7, 10, stride=8), :]
    trips = trips_of(live)
    source = [rows[pl.ds(32 + 4 + c, 2, stride=8), :] for c in range(3)]
    residual = [jnp.concatenate([moved[c, pl.ds(first + k, 1), :] for k in range(10)], axis=0) for c in range(3)]

    def tiles(box, x):
        layer, w = x + box // 2 - 2, box % 2
        inside = 0 <= layer < NX
        spot_ref = plane_wide if inside else out_wide
        base = (layer * 2 + w if inside else w) * TILE

        def scalar(k, part, n):
            if not inside:
                return out_keep[part * 6 + k, tile_at(n, base), :]
            if layer == 0 and k < 2:
                return edge_keep[part * 2 + k, tile_at(n, w * TILE), :]
            if layer == NX - 1 and k >= 4:
                return edge_keep[part * 2 + k - 4, tile_at(n, (2 + w) * TILE), :]
            return plane_keep[part * 6 + k, tile_at(n, base), :]

        def body(n, carry):
            for u in range(2):
                tile = n * 2 + u
                spot = [spot_ref[c, tile_at(tile, base), :] for c in range(3)]
                parts = []
                for k in range(6):
                    near = (box // 2 - 1) * 2 + k
                    delta = [spot[c] - row(rows, near * 8 + c) for c in range(3)]
                    moment = [row(rows, near * 8 + 4 + c) for c in range(3)]
                    parts.append(field_of(delta, scalar(k, 0, tile), scalar(k, 1, tile), moment))
                for c in range(3):
                    total[c, tile_at(tile, (box - 2) * TILE), :] = added([part[c] for part in parts])
            return carry

        lax.fori_loop(0, (trips[box, 0] + 1) // 2, body, 0)

    def sweep(boxes, moments):
        for c in range(3):
            rows[pl.ds(4 + c, 10, stride=8), :] = moments[c]
        for x in range(NX):

            @pl.when(x_me == x)
            def _():
                for box in boxes:
                    tiles(box, x)

        return [jnp.concatenate([lane_sums(total, c, box - 2) for box in boxes], axis=0) for c in range(3)]

    one = [pol * residual[c] for c in range(3)]
    fields = sweep(range(2, 8), one)
    two = []
    edge = jnp.zeros((2, TILE), F32)
    for c in range(3):
        value = pol[2:8] * (residual[c][2:8] + fields[c] + alone[2:8] * one[c][2:8])
        two.append(jnp.concatenate([edge, jnp.where(live[2:8] > 0.0, value, 0.0), edge], axis=0))
        two_ref[c, 0:10, :] = two[c]
    fields = sweep(range(4, 6), two)
    for c in range(3):
        value = pol[4:6] * (residual[c][4:6] + fields[c] + alone[4:6] * two_ref[c, 4:6, :])
        three = source[c] + jnp.where(live[4:6] > 0.0, value, 0.0)
        for w in range(2):
            new_ref[c : c + 1, w * TILE : (w + 1) * TILE] = three[w : w + 1]
            out_ref[c : c + 1, w * TILE : (w + 1) * TILE] = residual[c][4 + w : 5 + w]


VMEM = pl.BlockSpec(memory_space=pltpu.VMEM)
HBM = pl.BlockSpec(memory_space=pltpu.HBM)


def shape_of(shape):
    return shape if isinstance(shape, jax.ShapeDtypeStruct) else jax.ShapeDtypeStruct(shape, F32)


def call(body, ins, outs, scratch, cost, limit, name):
    return pl.pallas_call(
        body,
        in_specs=ins,
        out_specs=[VMEM] * len(outs),
        out_shape=[shape_of(shape) for shape in outs],
        scratch_shapes=[pltpu.VMEM(shape, F32) if isinstance(shape, tuple) else shape for shape in scratch],
        cost_estimate=pl.CostEstimate(flops=cost, bytes_accessed=1 << 20, transcendentals=0),
        compiler_params=pltpu.CompilerParams(vmem_limit_bytes=limit << 20),
        name=name,
    )


def device(group, box):
    return group * OWNERS + box


def rounds():
    plane = [
        [device(2 * y + core, z * NX + x) for y in range(NY) for x in range(NX)]
        for core in range(2)
        for z in range(OWNERS // NX)
    ]
    chip = [[device(2 * y, b), device(2 * y + 1, b)] for y in range(NY) for b in range(OWNERS)]
    up = [[(device(g, b), device(g, b + NX)) for b in range(OWNERS - NX)] for g in range(GROUPS)]
    down = [[(target, source) for source, target in pairs] for pairs in up]
    apart = [pair for g in range(GROUPS) for pair in (down[g] if g % 2 else up[g])]
    near_side = [(s, t) for pairs in up for s, t in pairs if s % NX < 2]
    near_side += [(s, t) for pairs in down for s, t in pairs if s % NX >= 2]
    return plane, chip, apart, near_side


PLANE_SETS, CHIP_SETS, APART, NEAR_SIDE = rounds()
OWN_ROWS = PLANE * 8 + 64
SIDE_ROWS = 256 + 64


def on_device(
    dipoles, perm_field, positions, polarizability, occupancy, far_boxes, far_class, far_count, far_scale, translations
):
    me = lax.axis_index("d").astype(jnp.int32)
    two = pltpu.SMEM((2,), jnp.int32)
    lists = pltpu.VMEM((2, ILIST), jnp.int32)
    [chunk] = call(
        first_kernel,
        [HBM] * 9,
        [(PLANE, CHUNK, TILE)],
        [(NTERM * 8, TILE), (CHUNK, TILE)]
        + [(3, 2 * TILE)] * 3
        + [(1, 2 * TILE), (2, ILIST), lists, lists, two, two, pltpu.SemaphoreType.DMA((9,))],
        1 << 20,
        60,
        "first",
    )(
        occupancy, far_count, dipoles, perm_field, positions, polarizability.reshape(1, 2 * TILE),
        far_boxes, far_class, far_scale,
    )
    block = lax.all_to_all(chunk, "d", 0, 0, axis_index_groups=PLANE_SETS, tiled=True)
    half = jax.ShapeDtypeStruct((CLASSES * 256, NTERM), BF16)
    t_high, t_low = call(prepare_kernel, [VMEM], [half, half], [], 1 << 28, 12, "prepare")(
        jnp.transpose(translations, (1, 0, 2))
    )
    mine = (me // (2 * OWNERS)) * NX
    core = (me // OWNERS) & 1
    near = lax.dynamic_slice(block, (mine, 8, 0), (NX, 16, TILE)).reshape(64, TILE)
    part = jnp.concatenate([block[:, 0:8, :].reshape(PLANE * 8, TILE), near], axis=0)
    part, t_high, t_low = lax.optimization_barrier((part, t_high, t_low))
    own = lax.all_gather(part, "d", axis_index_groups=CHIP_SETS, axis=0)
    edges = lax.dynamic_slice(own, (0, PLANE * 8 + 32 * (1 - core), 0), (2, 32, TILE)).reshape(64, TILE)
    away = jnp.concatenate([own[:, 0 : PLANE * 8].reshape(256, TILE), edges], axis=0)
    came = lax.ppermute(away, "d", APART)
    own = own.reshape(2 * OWN_ROWS, TILE)
    half = jax.ShapeDtypeStruct((8 * 176, TILE), BF16)
    sel, near_zero, wide, m_high, m_low, plane_keep = call(
        second_kernel,
        [VMEM],
        [(64, 192), (24, TILE), (4, 8 * TILE, TILE), half, half, (12, 8 * TILE, TILE)],
        [(TILE, TILE), (3, 8 * TILE, TILE), (NTERM * 8, TILE)],
        1 << 28,
        20,
        "second",
    )(block)
    came, sel = lax.optimization_barrier((came, sel))
    sides = lax.all_gather(came, "d", axis_index_groups=CHIP_SETS, axis=0).reshape(2 * SIDE_ROWS, TILE)
    residual, send, edge_keep = call(
        third_kernel,
        [VMEM] * 10,
        [(24, TILE), (12, TILE), (4, 4 * TILE, TILE)],
        [(256, TILE), (48, TILE), (48, TILE), (24, TILE), (TILE, TILE), (3, 4 * TILE, TILE)],
        1 << 28,
        16,
        "third",
    )(block, own, sides, sel, near_zero, wide, m_high, m_low, t_high, t_low)
    got = lax.ppermute(send, "d", NEAR_SIDE)
    rows, out_keep, out_wide = call(
        window_kernel,
        [VMEM] * 2,
        [(TILE, TILE), (12, 2 * TILE, TILE), (4, 2 * TILE, TILE)],
        [(TILE, TILE)],
        1 << 28,
        12,
        "window",
    )(block, sides)
    new, out = call(
        fourth_kernel,
        [VMEM] * 8,
        [(3, 2 * TILE), (3, 2 * TILE)],
        [(3, 16, TILE), (TILE, TILE), (3, 6 * TILE, TILE), (3, 16, TILE)],
        1 << 28,
        20,
        "fourth",
    )(rows, plane_keep, edge_keep, out_keep, wide, out_wide, residual, got)
    return new, out


def solution(mesh):
    flat = Mesh(mesh.devices.reshape(-1), ("d",))
    return jax.shard_map(
        on_device,
        mesh=flat,
        in_specs=(
            P(None, "d"), P(None, "d"), P(None, "d"), P("d"), P("d"), P("d", None), P("d", None), P("d"), P("d", None), P(),
        ),
        out_specs=(P(None, "d"), P(None, "d")),
        check_vma=False,
    )
```

profile of v0, /device:TPU:224, one launch (start us, length us, event | category | flops | bytes accessed | tf_op | source)
XLA Modules:
  0.0 45.9 jit_solution(16897892827309513814)
XLA Ops:
  0.6 2.0 %first.1 = f32[16,40,128]{2,1,0:T(8,128)} custom-call(s32[2]{0:T(128)} %occ_hbm.1, s32[2]{0:T(128)} %count_hbm.1, f32[3,256]{1,0:T(4,128)} %dip_hbm.1, f32[3,256]{1,0:T(4,128)} %perm_hbm.1, f32[3,256]{1,0:T(4,128)} %pos_hbm.1, f32[1,256]{1,0:T(1,128)} %bitcast.14, s32[2,189]{1,0:T(2,128)} %boxes_hbm.1, s32[2,189]{1,0:T(2,128)} %class_hbm.1, f32[2,189]{1,0:T(2,128)} %scale_hbm.1), custom_call_target="tpu_custom_call" | custom-call | flops 1048576 | bytes 1048576 | tf_op jit(solution)/shard_map/first/pallas_call | solution.py:541
  2.6 7.0 %all-to-all-start = ((f32[16,40,128]{2,1,0:T(8,128)}), f32[16,40,128]{2,1,0:T(8,128)S(1)}, u32[]{:S(2)}, u32[]{:S(2)}) async-start(f32[16,40,128]{2,1,0:T(8,128)} %first.1), calls=%async_computation | async-start | bytes 655360 | tf_op jit(solution)/shard_map/all_to_all | solution.py:555
  9.7 0.0 copy-start
  9.7 1.3 %copy-done = f32[8,165,165]{2,0,1:T(8,128)S(1)} copy-done((f32[8,165,165]{2,0,1:T(8,128)S(1)}, f32[8,165,165]{2,0,1:T(8,128)}, u32[]{:S(2)}) %copy-start) | copy-done | bytes 871224
  11.1 0.8 %prepare.1 = (bf16[2048,165]{1,0:T(8,128)(2,1)S(1)}, bf16[2048,165]{1,0:T(8,128)(2,1)S(1)}) custom-call(f32[165,8,165]{2,1,0:T(8,128)S(1)} %bitcast.10), custom_call_target="tpu_custom_call" | custom-call | flops 268435456 | bytes 1048576 | tf_op jit(solution)/shard_map/prepare/pallas_call | solution.py:557
  11.8 7.3 %all-to-all-done.block_ref = f32[16,40,128]{2,1,0:T(8,128)S(1)} async-done(((f32[16,40,128]{2,1,0:T(8,128)}), f32[16,40,128]{2,1,0:T(8,128)S(1)}, u32[]{:S(2)}, u32[]{:S(2)}) %all-to-all-start) | async-done | bytes 327712 | tf_op jit(solution)/shard_map/all_to_all | solution.py:555
  19.1 1.9 %all-gather.own_ref = f32[384,128]{1,0:T(8,128)S(1)} all-gather(f32[192,128]{1,0:T(8,128)S(1)} %pad_maximum_fusion.1), channel_id=2, replica_groups={{0,64},{1,65},{2,66},{3,67},{4,68},{5,69},{6,70},{7,71},{8,72},{9,73},{..., dimensions={0}, use_global_device_ids=true | all-gather | bytes 294912 | tf_op jit(solution)/shard_map/all_gather | solution.py:565
  21.1 5.0 %collective-permute-start = (f32[320,128]{1,0:T(8,128)S(1)}, f32[320,128]{1,0:T(8,128)S(1)}, u32[]{:S(2)}, u32[]{:S(2)}) collective-permute-start(f32[320,128]{1,0:T(8,128)S(1)} %pad_maximum_fusion), channel_id=1, source_target_pairs={{0,4},{1,5},{2,6},{3,7},{4,8},{5,9},{6,10},{7,11},{8,12},{9,13},{1... | collective-permute-start | bytes 491528 | tf_op jit(solution)/shard_map/ppermute | solution.py:568
  26.2 5.7 %second.1 = (f32[64,192]{1,0:T(8,128)S(1)}, f32[24,128]{1,0:T(8,128)S(1)}, f32[4,1024,128]{2,1,0:T(8,128)S(1)}, bf16[1408,128]{1,0:T(8,128)(2,1)S(1)}, bf16[1408...) custom-call(f32[16,40,128]{2,1,0:T(8,128)S(1)} %all-to-all-done.block_ref), custom_call_target="tpu_custom_call" | custom-call | flops 268435456 | bytes 1048576 | tf_op jit(solution)/shard_map/second/pallas_call | solution.py:571
  31.8 0.0 collective-permute-done
  31.8 2.0 %all-gather.1.sides_ref = f32[640,128]{1,0:T(8,128)S(1)} all-gather(f32[320,128]{1,0:T(8,128)S(1)} %collective-permute-done), channel_id=3, replica_groups={{0,64},{1,65},{2,66},{3,67},{4,68},{5,69},{6,70},{7,71},{8,72},{9,73},{..., dimensions={0}, use_global_device_ids=true | all-gather | bytes 491520 | tf_op jit(solution)/shard_map/all_gather | solution.py:581
  33.9 2.7 %third.1 = (f32[24,128]{1,0:T(8,128)S(1)}, f32[12,128]{1,0:T(8,128)S(1)}, f32[4,512,128]{2,1,0:T(8,128)S(1)}) custom-call(f32[16,40,128]{2,1,0:T(8,128)S(1)} %all-to-all-done.block_ref, f32[384,128]{1,0:T(8,128)S(1)} %all-gather.own_ref, f32[640,128]{1,0:T(8,128)S(1)} %all-gather.1.sides_ref, f32[64,192]{1,0:T(8,128)S(1)} %get-tuple-element.28.sel_ref, ...), custom_call_target="tpu_custom_call" | custom-call | flops 268435456 | bytes 1048576 | tf_op jit(solution)/shard_map/third/pallas_call | solution.py:582
  36.6 2.6 %collective-permute-start.1 = (f32[12,128]{1,0:T(8,128)S(1)}, f32[12,128]{1,0:T(8,128)S(1)}, u32[]{:S(2)}, u32[]{:S(2)}) collective-permute-start(f32[12,128]{1,0:T(8,128)S(1)} %get-tuple-element.39), channel_id=1, source_target_pairs={{0,4},{1,5},{4,8},{5,9},{8,12},{9,13},{12,16},{13,17},{16,20},{17,... | collective-permute-start | bytes 18440 | tf_op jit(solution)/shard_map/ppermute | solution.py:591
  39.2 1.0 %window.1 = (f32[128,128]{1,0:T(8,128)S(1)}, f32[12,256,128]{2,1,0:T(8,128)S(1)}, f32[4,256,128]{2,1,0:T(8,128)S(1)}) custom-call(f32[16,40,128]{2,1,0:T(8,128)S(1)} %all-to-all-done.block_ref, f32[640,128]{1,0:T(8,128)S(1)} %all-gather.1.sides_ref), custom_call_target="tpu_custom_call" | custom-call | flops 268435456 | bytes 1048576 | tf_op jit(solution)/shard_map/window/pallas_call | solution.py:592
  40.2 1.9 %collective-permute-done.1.got_ref = f32[12,128]{1,0:T(8,128)S(1)} collective-permute-done((f32[12,128]{1,0:T(8,128)S(1)}, f32[12,128]{1,0:T(8,128)S(1)}, u32[]{:S(2)}, u32[]{:S(2)}) %collective-permute-start.1) | collective-permute-done | bytes 6176 | tf_op jit(solution)/shard_map/ppermute | solution.py:591
  42.1 3.8 %fourth.1 = (f32[3,256]{1,0:T(4,128)}, f32[3,256]{1,0:T(4,128)}) custom-call(f32[128,128]{1,0:T(8,128)S(1)} %get-tuple-element.26.rows_ref, f32[12,1024,128]{2,1,0:T(8,128)S(1)} %get-tuple-element.27.plane_keep, f32[4,512,128]{2,1,0:T(8,128)S(1)} %get-tuple-element.35.edge_keep, f32[12,256,128]{2,1,0:T(8,128)S(1)} %get-tuple-element.36.out_keep, ...), custom_call_target="tpu_custom_call" | custom-call | flops 268435456 | bytes 1048576 | tf_op jit(solution)/shard_map/fourth/pallas_call | solution.py:601
  (6 shorter events, 0.1 us)
Async XLA Ops:
  2.6 16.4 %all-to-all-start = ((f32[16,40,128]{2,1,0:T(8,128)}), f32[16,40,128]{2,1,0:T(8,128)S(1)}, u32[]{:S(2)}, u32[]{:S(2)}) async-start(f32[16,40,128]{2,1,0:T(8,128)} %first.1), calls=%async_computation | async-start | bytes 655360 | tf_op jit(solution)/shard_map/all_to_all | solution.py:555
  9.7 1.3 %copy-start = (f32[8,165,165]{2,0,1:T(8,128)S(1)}, f32[8,165,165]{2,0,1:T(8,128)}, u32[]{:S(2)}) copy-start(f32[8,165,165]{2,0,1:T(8,128)} %param.19) | copy-start | bytes 2613604
  21.1 10.7 %collective-permute-start = (f32[320,128]{1,0:T(8,128)S(1)}, f32[320,128]{1,0:T(8,128)S(1)}, u32[]{:S(2)}, u32[]{:S(2)}) collective-permute-start(f32[320,128]{1,0:T(8,128)S(1)} %pad_maximum_fusion), channel_id=1, source_target_pairs={{0,4},{1,5},{2,6},{3,7},{4,8},{5,9},{6,10},{7,11},{8,12},{9,13},{1... | collective-permute-start | bytes 491528 | tf_op jit(solution)/shard_map/ppermute | solution.py:568
  36.6 5.5 %collective-permute-start.1 = (f32[12,128]{1,0:T(8,128)S(1)}, f32[12,128]{1,0:T(8,128)S(1)}, u32[]{:S(2)}, u32[]{:S(2)}) collective-permute-start(f32[12,128]{1,0:T(8,128)S(1)} %get-tuple-element.39), channel_id=1, source_target_pairs={{0,4},{1,5},{4,8},{5,9},{8,12},{9,13},{12,16},{13,17},{16,20},{17,... | collective-permute-start | bytes 18440 | tf_op jit(solution)/shard_map/ppermute | solution.py:591
where the time goes:
time: 45.8 us; the launch traced here: 45.9 us
  Pallas kernels  15.8 us (34%)
  starting transfers between devices  14.7 us (32%)
  waiting for transfers between devices  9.19 us (20%)
  blocking collectives  3.99 us (9%)
  local copies, waits for them, and re-layouts  1.36 us (3%)
  between operations  0.77 us (2%)
    all_to_all x1, waiting for transfers between devices, on_device(): lax.all_to_all(chunk, 'd', 0, 0, axis_index_groups=PLANE_SETS, tiled=True)  7.25 us
    all_to_all x1, starting transfers between devices, on_device(): lax.all_to_all(chunk, 'd', 0, 0, axis_index_groups=PLANE_SETS, tiled=True)  7.05 us
    pallas_call x1, Pallas kernels, on_device(): call(second_kernel, [VMEM], [(64, 192), (24, TILE), (4, 8 * TILE, TILE),...  5.66 us
    ppermute x1, starting transfers between devices, on_device(): came = lax.ppermute(away, 'd', APART)  5.04 us
    pallas_call x1, Pallas kernels, on_device(): call(fourth_kernel, [VMEM] * 8, [(3, 2 * TILE), (3, 2 * TILE)], [(3, 16,...  3.76 us
    pallas_call x1, Pallas kernels, on_device(): call(third_kernel, [VMEM] * 10, [(24, TILE), (12, TILE), (4, 4 * TILE, TI...  2.67 us
    ppermute x1, starting transfers between devices, on_device(): got = lax.ppermute(send, 'd', NEAR_SIDE)  2.62 us
    all_gather x1, blocking collectives, on_device(): lax.all_gather(came, 'd', axis_index_groups=CHIP_SETS, axis=0)  2.04 us
  transfers between devices with their start and end apart: 3, of which 2 were waited for; matrix products, arithmetic and copies ran while one was open for 0% of the time, Pallas kernels for 16%

commit v1 on v0

--- a/solution.py
+++ b/solution.py
@@ -198,9 +198,7 @@
             wide_ref[f, slot * TILE : (slot + 1) * TILE, :] = -value if f == 3 else value
 
 
-def near_boxes(total_ref, slots, wide_ref, targets, trips, rows_ref, sources, keep_ref, first_kept):
-    half = keep_ref.shape[0] // 2
-
+def near_boxes(total_ref, slots, wide_ref, targets, trips, rows_ref, sources, keep_ref):
     def body(n, carry):
         mine = [[wide_ref[f, tile_at(n, target * TILE), :] for f in range(4)] for target in targets]
         parts = [[] for _ in targets]
@@ -209,9 +207,10 @@
             for i, spot in enumerate(mine):
                 delta = [spot[c] - where[c] for c in range(3)]
                 radial, direct = scalars(delta, spot[3] * where[3])
-                kept = tile_at(n, slots[i] * TILE)
-                keep_ref[first_kept + k, kept, :] = radial
-                keep_ref[half + first_kept + k, kept, :] = direct
+                if keep_ref is not None:
+                    kept = tile_at(n, slots[i] * TILE)
+                    keep_ref[k, kept, :] = radial
+                    keep_ref[6 + k, kept, :] = direct
                 parts[i].append(field_of(delta, radial, direct, where[4:7]))
         for i, slot in enumerate(slots):
             for c in range(3):
@@ -256,10 +255,21 @@
         high, low = halves(mono[pl.ds(k, NTERM, stride=8), :])
         m_high_ref[k * 176 : k * 176 + NTERM, :] = high
         m_low_ref[k * 176 : k * 176 + NTERM, :] = low
-    for box in range(8):
-        low, high = max(box // 2 - 1, 0), min(box // 2 + 1, NX - 1)
-        sources = range(low * 2, high * 2 + 2)
-        near_boxes(total, [box], wide, [box], trips[box, 0], rows, sources, keep, low * 2 - (box // 2 - 1) * 2)
+    x_me = own_place()[2]
+    near_ref[...] = jnp.zeros_like(near_ref)
+    for box in range(2, 6):
+        first = (box // 2 - 1) * 2
+        near_boxes(total, [box - 2], wide, [box], trips[box, 0], rows, range(first, first + 6), keep)
+    for sent, boxes, sources in ((x_me < 2, (6, 7), range(4, 8)), (x_me >= 2, (0, 1), range(4))):
+
+        @pl.when(sent)
+        def _():
+            for w, box in enumerate(boxes):
+                near_boxes(total, [4 + w], wide, [box], trips[box, 0], rows, sources, None)
+            for c in range(3):
+                for w, box in enumerate(boxes):
+                    near_ref[c * 8 + box : c * 8 + box + 1, :] = lane_sums(total, c, 4 + w)
+
     spot = lax.broadcasted_iota(jnp.int32, (192, TILE), 0)
     kinds = lax.broadcasted_iota(jnp.int32, (CLASSES, TILE), 0)
     side = lax.broadcasted_iota(jnp.int32, (CLASSES, TILE), 1) >> 6
@@ -287,13 +297,13 @@
             tail = second[w * 16 : w * 16 + 16]
             sel_ref[k * 8 : k * 8 + 8, :] = (first[w][0:8] + tail[0:8]) + (first[w][8:16] + tail[8:16])
     for c in range(3):
-        for box in range(8):
-            near_ref[c * 8 + box : c * 8 + box + 1, :] = lane_sums(total, c, box)
+        for box in range(2, 6):
+            near_ref[c * 8 + box : c * 8 + box + 1, :] = lane_sums(total, c, box - 2)
 
 
 def third_kernel(
     block_ref, own_ref, sides_ref, sel_ref, near_ref, wide_ref, m_high_ref, m_low_ref, t_high_ref, t_low_ref,
-    res_ref, send_ref, keep, summed, head, rest, far, rows, total,
+    res_ref, send_ref, summed, head, rest, far, rows, total,
 ):
     core, _, x_me, mine = own_place()
     sel_high, sel_low = halves(sel_ref[...])
@@ -337,9 +347,13 @@
     root = root_of(pol)
     trips = trips_of(live)
     write_fields(rows, 12, px, py, pz, root, -1)
-    for slots, boxes, sources in (((0, 1), (0, 1), (0, 1)), ((2, 3), (6, 7), (10, 11))):
-        most = jnp.maximum(trips[boxes[0], 0], trips[boxes[1], 0])
-        near_boxes(total, slots, wide_ref, boxes, most, rows, sources, keep, 0)
+    for sent, boxes, sources in ((x_me < 2, (6, 7), (10, 11)), (x_me >= 2, (0, 1), (0, 1))):
+
+        @pl.when(sent)
+        def _():
+            most = jnp.maximum(trips[boxes[0], 0], trips[boxes[1], 0])
+            near_boxes(total, (0, 1), wide_ref, boxes, most, rows, sources, None)
+
     for k in range(8):
         left = jnp.concatenate([head[pl.ds(k, 6, stride=8), :], rest[pl.ds(k, 6, stride=8), :][:, 0:REST]], axis=1)
         left = left.astype(BF16)
@@ -349,13 +363,13 @@
         for c in range(3):
             far[c * 8 + k : c * 8 + k + 1, :] = value[c : c + 1]
     alone = self_term(root[2:10])
-    nothing = jnp.zeros((4, TILE), F32)
+    nothing = jnp.zeros((6, TILE), F32)
     for c in range(3):
         perm = jnp.concatenate(
             [block_ref[mine + x, 24 + w * 3 + c : 25 + w * 3 + c, :] for x in range(NX) for w in range(2)], axis=0
         )
-        ends = [lane_sums(total, c, slot) for slot in range(4)]
-        edge = jnp.concatenate(ends[0:2] + [nothing] + ends[2:4], axis=0)
+        ends = [lane_sums(total, c, slot) for slot in range(2)]
+        edge = jnp.where(x_me < 2, jnp.concatenate([nothing] + ends, axis=0), jnp.concatenate(ends + [nothing], axis=0))
         near_zero = near_ref[c * 8 : c * 8 + 8, :] + edge + alone * source[c]
         res_ref[c * 8 : c * 8 + 8, :] = jnp.where(
             live > 0.0, perm + far[c * 8 : c * 8 + 8, :] + near_zero - source[c] / pol[2:10], 0.0
@@ -366,7 +380,7 @@
             send_ref[c * 4 + k : c * 4 + k + 1, :] = res_ref[pl.ds(c * 8 + first + k, 1), :]
 
 
-def window_kernel(block_ref, sides_ref, rows, keep, edge, every):
+def window_kernel(block_ref, sides_ref, wide_ref, rows, keep, edge, late_keep, late_ref, every, total):
     core, _, x_me, mine = own_place()
     first = x_me * 2
     every[0:32, :] = sides_ref[pl.ds(pl.multiple_of(256 + 32 * core, 8), 32), :]
@@ -386,6 +400,21 @@
     rows[96:106, :] = self_term(root)
     trips = trips_of(live)
     write_fields(rows, 10, px, py, pz, root, x_me - 2)
+    for x, layer in enumerate((2, 1, 3, 2)):
+
+        @pl.when(x_me == x)
+        def _():
+            plane_box = 0 if x < 2 else 6
+            first_source = (layer - 1) * 2
+            for w in range(2):
+                sources = range(first_source, first_source + 6)
+                many = trips[layer * 2 + w, 0]
+                near_boxes(total, [w], wide_ref, [plane_box + w], many, rows, sources, late_keep)
+            for w in range(2):
+                alive = live[layer * 2 + w : layer * 2 + w + 1] > 0.0
+                for c in range(3):
+                    late_ref[c * 2 + w : c * 2 + w + 1, :] = jnp.where(alive, lane_sums(total, c, w), 0.0)
+
     for outside, layer in ((x_me == 0, 1), (x_me == NX - 1, 3)):
 
         @pl.when(outside)
@@ -410,7 +439,7 @@
 
 
 def fourth_kernel(
-    rows_ref, plane_keep, edge_keep, out_keep, plane_wide, out_wide, res_ref, got_ref, new_ref, out_ref,
+    rows_ref, plane_keep, late_keep, late_ref, out_keep, plane_wide, out_wide, res_ref, got_ref, new_ref, out_ref,
     moved, rows, total, two_ref,
 ):
     x_me = own_place()[2]
@@ -420,6 +449,9 @@
         moved[c, 0:4, :] = got
         moved[c, 4:12, :] = res_ref[c * 8 : c * 8 + 8, :]
         moved[c, 12:16, :] = got
+        for w in range(2):
+            at = pl.ds(jnp.where(x_me < 2, 4, 10) + w, 1)
+            moved[c, at, :] = moved[c, at, :] + late_ref[c * 2 + w : c * 2 + w + 1, :]
     rows[...] = rows_ref[...]
     pol, alone = rows[80:90, :], rows[96:106, :]
     live = rows[pl.ds(7, 10, stride=8), :]
@@ -436,11 +468,9 @@
         def scalar(k, part, n):
             if not inside:
                 return out_keep[part * 6 + k, tile_at(n, base), :]
-            if layer == 0 and k < 2:
-                return edge_keep[part * 2 + k, tile_at(n, w * TILE), :]
-            if layer == NX - 1 and k >= 4:
-                return edge_keep[part * 2 + k - 4, tile_at(n, (2 + w) * TILE), :]
-            return plane_keep[part * 6 + k, tile_at(n, base), :]
+            if layer == (0 if x < 2 else NX - 1):
+                return late_keep[part * 6 + k, tile_at(n, w * TILE), :]
+            return plane_keep[part * 6 + k, tile_at(n, base - 2 * TILE), :]
 
         def body(n, carry):
             for u in range(2):
@@ -571,42 +601,42 @@
     sel, near_zero, wide, m_high, m_low, plane_keep = call(
         second_kernel,
         [VMEM],
-        [(64, 192), (24, TILE), (4, 8 * TILE, TILE), half, half, (12, 8 * TILE, TILE)],
-        [(TILE, TILE), (3, 8 * TILE, TILE), (NTERM * 8, TILE)],
+        [(64, 192), (24, TILE), (4, 8 * TILE, TILE), half, half, (12, 4 * TILE, TILE)],
+        [(TILE, TILE), (3, 6 * TILE, TILE), (NTERM * 8, TILE)],
         1 << 28,
         20,
         "second",
     )(block)
     came, sel = lax.optimization_barrier((came, sel))
     sides = lax.all_gather(came, "d", axis_index_groups=CHIP_SETS, axis=0).reshape(2 * SIDE_ROWS, TILE)
-    residual, send, edge_keep = call(
+    residual, send = call(
         third_kernel,
         [VMEM] * 10,
-        [(24, TILE), (12, TILE), (4, 4 * TILE, TILE)],
-        [(256, TILE), (48, TILE), (48, TILE), (24, TILE), (TILE, TILE), (3, 4 * TILE, TILE)],
+        [(24, TILE), (12, TILE)],
+        [(256, TILE), (48, TILE), (48, TILE), (24, TILE), (TILE, TILE), (3, 2 * TILE, TILE)],
         1 << 28,
         16,
         "third",
     )(block, own, sides, sel, near_zero, wide, m_high, m_low, t_high, t_low)
     got = lax.ppermute(send, "d", NEAR_SIDE)
-    rows, out_keep, out_wide = call(
+    rows, out_keep, out_wide, late_keep, late = call(
         window_kernel,
-        [VMEM] * 2,
-        [(TILE, TILE), (12, 2 * TILE, TILE), (4, 2 * TILE, TILE)],
-        [(TILE, TILE)],
+        [VMEM] * 3,
+        [(TILE, TILE), (12, 2 * TILE, TILE), (4, 2 * TILE, TILE), (12, 2 * TILE, TILE), (8, TILE)],
+        [(TILE, TILE), (3, 2 * TILE, TILE)],
         1 << 28,
-        12,
+        16,
         "window",
-    )(block, sides)
+    )(block, sides, wide)
     new, out = call(
         fourth_kernel,
-        [VMEM] * 8,
+        [VMEM] * 9,
         [(3, 2 * TILE), (3, 2 * TILE)],
         [(3, 16, TILE), (TILE, TILE), (3, 6 * TILE, TILE), (3, 16, TILE)],
         1 << 28,
         20,
         "fourth",
-    )(rows, plane_keep, edge_keep, out_keep, wide, out_wide, residual, got)
+    )(rows, plane_keep, late_keep, late, out_keep, wide, out_wide, residual, got)
     return new, out
 
 

time: 45.8 us -> 44.8 us (0.978)
  starting transfers between devices: 14.7 us -> 17.3 us
  Pallas kernels: 15.8 us -> 13.8 us
  waiting for transfers between devices: 9.19 us -> 7.26 us
    ppermute x1, starting transfers between devices: 2.62 us -> 5.2 us  [on_device(): got = lax.ppermute(send, 'd', NEAR_SIDE)]
    pallas_call x1, Pallas kernels: 5.66 us -> 3.61 us  [on_device(): call(second_kernel, [VMEM], [(64, 192), (24, TILE), (4, 8 * TILE, TILE),...]
    ppermute x1, waiting for transfers between devices: 1.93 us -> 0.01 us  [on_device(): got = lax.ppermute(send, 'd', NEAR_SIDE)]
  transfers between devices with their start and end apart: 3 -> 3, of which waited for: 2 -> 1; matrix products, arithmetic and copies ran while one was open for 0% -> 0% of each run, Pallas kernels for 16% -> 15%
where the time goes in v1:
time: 44.8 us; the launch traced here: 44.5 us
  starting transfers between devices  17.3 us (39%)
  Pallas kernels  13.8 us (31%)
  waiting for transfers between devices  7.26 us (16%)
  blocking collectives  3.99 us (9%)
  local copies, waits for them, and re-layouts  1.36 us (3%)
  between operations  0.76 us (2%)
    all_to_all x1, waiting for transfers between devices, on_device(): lax.all_to_all(chunk, 'd', 0, 0, axis_index_groups=PLANE_SETS, tiled=True)  7.25 us
    all_to_all x1, starting transfers between devices, on_device(): lax.all_to_all(chunk, 'd', 0, 0, axis_index_groups=PLANE_SETS, tiled=True)  7.05 us
    ppermute x1, starting transfers between devices, on_device(): got = lax.ppermute(send, 'd', NEAR_SIDE)  5.2 us
    ppermute x1, starting transfers between devices, on_device(): came = lax.ppermute(away, 'd', APART)  5.04 us
    pallas_call x1, Pallas kernels, on_device(): call(second_kernel, [VMEM], [(64, 192), (24, TILE), (4, 8 * TILE, TILE),...  3.61 us
    pallas_call x1, Pallas kernels, on_device(): call(fourth_kernel, [VMEM] * 9, [(3, 2 * TILE), (3, 2 * TILE)], [(3, 16,...  3.39 us
    pallas_call x1, Pallas kernels, on_device(): call(window_kernel, [VMEM] * 3, [(TILE, TILE), (12, 2 * TILE, TILE), (4,...  2.29 us
    all_gather x1, blocking collectives, on_device(): lax.all_gather(came, 'd', axis_index_groups=CHIP_SETS, axis=0)  2.04 us
  transfers between devices with their start and end apart: 3, of which 1 were waited for; matrix products, arithmetic and copies ran while one was open for 0% of the time, Pallas kernels for 15%

profile of v1, /device:TPU:224, one launch (start us, length us, event | category | flops | bytes accessed | tf_op | source)
XLA Modules:
  0.0 44.5 jit_solution(15716592463281871394)
XLA Ops:
  0.6 2.0 %first.1 = f32[16,40,128]{2,1,0:T(8,128)} custom-call(s32[2]{0:T(128)} %occ_hbm.1, s32[2]{0:T(128)} %count_hbm.1, f32[3,256]{1,0:T(4,128)} %dip_hbm.1, f32[3,256]{1,0:T(4,128)} %perm_hbm.1, f32[3,256]{1,0:T(4,128)} %pos_hbm.1, f32[1,256]{1,0:T(1,128)} %bitcast.14, s32[2,189]{1,0:T(2,128)} %boxes_hbm.1, s32[2,189]{1,0:T(2,128)} %class_hbm.1, f32[2,189]{1,0:T(2,128)} %scale_hbm.1), custom_call_target="tpu_custom_call" | custom-call | flops 1048576 | bytes 1048576 | tf_op jit(solution)/shard_map/first/pallas_call | solution.py:571
  2.6 7.0 %all-to-all-start = ((f32[16,40,128]{2,1,0:T(8,128)}), f32[16,40,128]{2,1,0:T(8,128)S(1)}, u32[]{:S(2)}, u32[]{:S(2)}) async-start(f32[16,40,128]{2,1,0:T(8,128)} %first.1), calls=%async_computation | async-start | bytes 655360 | tf_op jit(solution)/shard_map/all_to_all | solution.py:585
  9.7 0.0 copy-start
  9.7 1.3 %copy-done = f32[8,165,165]{2,0,1:T(8,128)S(1)} copy-done((f32[8,165,165]{2,0,1:T(8,128)S(1)}, f32[8,165,165]{2,0,1:T(8,128)}, u32[]{:S(2)}) %copy-start) | copy-done | bytes 871224
  11.1 0.8 %prepare.1 = (bf16[2048,165]{1,0:T(8,128)(2,1)S(1)}, bf16[2048,165]{1,0:T(8,128)(2,1)S(1)}) custom-call(f32[165,8,165]{2,1,0:T(8,128)S(1)} %bitcast.10), custom_call_target="tpu_custom_call" | custom-call | flops 268435456 | bytes 1048576 | tf_op jit(solution)/shard_map/prepare/pallas_call | solution.py:587
  11.8 7.3 %all-to-all-done.block_ref = f32[16,40,128]{2,1,0:T(8,128)S(1)} async-done(((f32[16,40,128]{2,1,0:T(8,128)}), f32[16,40,128]{2,1,0:T(8,128)S(1)}, u32[]{:S(2)}, u32[]{:S(2)}) %all-to-all-start) | async-done | bytes 327712 | tf_op jit(solution)/shard_map/all_to_all | solution.py:585
  19.1 1.9 %all-gather.own_ref = f32[384,128]{1,0:T(8,128)S(1)} all-gather(f32[192,128]{1,0:T(8,128)S(1)} %pad_maximum_fusion.1), channel_id=2, replica_groups={{0,64},{1,65},{2,66},{3,67},{4,68},{5,69},{6,70},{7,71},{8,72},{9,73},{..., dimensions={0}, use_global_device_ids=true | all-gather | bytes 294912 | tf_op jit(solution)/shard_map/all_gather | solution.py:595
  21.1 5.0 %collective-permute-start = (f32[320,128]{1,0:T(8,128)S(1)}, f32[320,128]{1,0:T(8,128)S(1)}, u32[]{:S(2)}, u32[]{:S(2)}) collective-permute-start(f32[320,128]{1,0:T(8,128)S(1)} %pad_maximum_fusion), channel_id=1, source_target_pairs={{0,4},{1,5},{2,6},{3,7},{4,8},{5,9},{6,10},{7,11},{8,12},{9,13},{1... | collective-permute-start | bytes 491528 | tf_op jit(solution)/shard_map/ppermute | solution.py:598
  26.2 3.6 %second.1 = (f32[64,192]{1,0:T(8,128)S(1)}, f32[24,128]{1,0:T(8,128)S(1)}, f32[4,1024,128]{2,1,0:T(8,128)S(1)}, bf16[1408,128]{1,0:T(8,128)(2,1)S(1)}, bf16[1408...) custom-call(f32[16,40,128]{2,1,0:T(8,128)S(1)} %all-to-all-done.block_ref), custom_call_target="tpu_custom_call" | custom-call | flops 268435456 | bytes 1048576 | tf_op jit(solution)/shard_map/second/pallas_call | solution.py:601
  29.8 0.0 collective-permute-done
  29.8 2.0 %all-gather.1.sides_ref = f32[640,128]{1,0:T(8,128)S(1)} all-gather(f32[320,128]{1,0:T(8,128)S(1)} %collective-permute-done), channel_id=3, replica_groups={{0,64},{1,65},{2,66},{3,67},{4,68},{5,69},{6,70},{7,71},{8,72},{9,73},{..., dimensions={0}, use_global_device_ids=true | all-gather | bytes 491520 | tf_op jit(solution)/shard_map/all_gather | solution.py:611
  31.8 1.7 %third.1 = (f32[24,128]{1,0:T(8,128)S(1)}, f32[12,128]{1,0:T(8,128)S(1)}) custom-call(f32[16,40,128]{2,1,0:T(8,128)S(1)} %all-to-all-done.block_ref, f32[384,128]{1,0:T(8,128)S(1)} %all-gather.own_ref, f32[640,128]{1,0:T(8,128)S(1)} %all-gather.1.sides_ref, f32[64,192]{1,0:T(8,128)S(1)} %get-tuple-element.34.sel_ref, ...), custom_call_target="tpu_custom_call" | custom-call | flops 268435456 | bytes 1048576 | tf_op jit(solution)/shard_map/third/pallas_call | solution.py:612
  33.6 5.2 %collective-permute-start.1 = (f32[12,128]{1,0:T(8,128)S(1)}, f32[12,128]{1,0:T(8,128)S(1)}, u32[]{:S(2)}, u32[]{:S(2)}) collective-permute-start(f32[12,128]{1,0:T(8,128)S(1)} %get-tuple-element.41), channel_id=1, source_target_pairs={{0,4},{1,5},{4,8},{5,9},{8,12},{9,13},{12,16},{13,17},{16,20},{17,... | collective-permute-start | bytes 18440 | tf_op jit(solution)/shard_map/ppermute | solution.py:621
  38.8 2.3 %window.1 = (f32[128,128]{1,0:T(8,128)S(1)}, f32[12,256,128]{2,1,0:T(8,128)S(1)}, f32[4,256,128]{2,1,0:T(8,128)S(1)}, f32[12,256,128]{2,1,0:T(8,128)S(1)}, f32[8,128]{1,0:T(8,128)S(1)}) custom-call(f32[16,40,128]{2,1,0:T(8,128)S(1)} %all-to-all-done.block_ref, f32[640,128]{1,0:T(8,128)S(1)} %all-gather.1.sides_ref, ...), custom_call_target="tpu_custom_call" | custom-call | flops 268435456 | bytes 1048576 | tf_op jit(solution)/shard_map/window/pallas_call | solution.py:622
  41.1 0.0 collective-permute-done.1.got_ref
  41.1 3.4 %fourth.1 = (f32[3,256]{1,0:T(4,128)}, f32[3,256]{1,0:T(4,128)}) custom-call(f32[128,128]{1,0:T(8,128)S(1)} %get-tuple-element.28.rows_ref, f32[12,512,128]{2,1,0:T(8,128)S(1)} %get-tuple-element.29.plane_keep, f32[12,256,128]{2,1,0:T(8,128)S(1)} %get-tuple-element.30.late_keep, f32[8,128]{1,0:T(8,128)S(1)} %get-tuple-element.31.late_ref, ...), custom_call_target="tpu_custom_call" | custom-call | flops 268435456 | bytes 1048576 | tf_op jit(solution)/shard_map/fourth/pallas_call | solution.py:631
  (6 shorter events, 0.1 us)
Async XLA Ops:
  2.6 16.4 %all-to-all-start = ((f32[16,40,128]{2,1,0:T(8,128)}), f32[16,40,128]{2,1,0:T(8,128)S(1)}, u32[]{:S(2)}, u32[]{:S(2)}) async-start(f32[16,40,128]{2,1,0:T(8,128)} %first.1), calls=%async_computation | async-start | bytes 655360 | tf_op jit(solution)/shard_map/all_to_all | solution.py:585
  9.7 1.3 %copy-start = (f32[8,165,165]{2,0,1:T(8,128)S(1)}, f32[8,165,165]{2,0,1:T(8,128)}, u32[]{:S(2)}) copy-start(f32[8,165,165]{2,0,1:T(8,128)} %param.19) | copy-start | bytes 2613604
  21.1 8.7 %collective-permute-start = (f32[320,128]{1,0:T(8,128)S(1)}, f32[320,128]{1,0:T(8,128)S(1)}, u32[]{:S(2)}, u32[]{:S(2)}) collective-permute-start(f32[320,128]{1,0:T(8,128)S(1)} %pad_maximum_fusion), channel_id=1, source_target_pairs={{0,4},{1,5},{2,6},{3,7},{4,8},{5,9},{6,10},{7,11},{8,12},{9,13},{1... | collective-permute-start | bytes 491528 | tf_op jit(solution)/shard_map/ppermute | solution.py:598
  33.6 7.5 %collective-permute-start.1 = (f32[12,128]{1,0:T(8,128)S(1)}, f32[12,128]{1,0:T(8,128)S(1)}, u32[]{:S(2)}, u32[]{:S(2)}) collective-permute-start(f32[12,128]{1,0:T(8,128)S(1)} %get-tuple-element.41), channel_id=1, source_target_pairs={{0,4},{1,5},{4,8},{5,9},{8,12},{9,13},{12,16},{13,17},{16,20},{17,... | collective-permute-start | bytes 18440 | tf_op jit(solution)/shard_map/ppermute | solution.py:621

commit v2 on v1

--- a/solution.py
+++ b/solution.py
@@ -187,7 +187,8 @@
 
 def trips_of(live):
     count = jnp.sum(live, axis=1, keepdims=True)
-    return ((count + 7.0) * 0.125).astype(jnp.int32)
+    tiles = ((count + 7.0) * 0.125).astype(jnp.int32)
+    return [tiles[k, 0] for k in range(live.shape[0])]
 
 
 def spread(wide_ref, cols, boxes, fields):
@@ -259,13 +260,13 @@
     near_ref[...] = jnp.zeros_like(near_ref)
     for box in range(2, 6):
         first = (box // 2 - 1) * 2
-        near_boxes(total, [box - 2], wide, [box], trips[box, 0], rows, range(first, first + 6), keep)
+        near_boxes(total, [box - 2], wide, [box], trips[box], rows, range(first, first + 6), keep)
     for sent, boxes, sources in ((x_me < 2, (6, 7), range(4, 8)), (x_me >= 2, (0, 1), range(4))):
 
         @pl.when(sent)
         def _():
             for w, box in enumerate(boxes):
-                near_boxes(total, [4 + w], wide, [box], trips[box, 0], rows, sources, None)
+                near_boxes(total, [4 + w], wide, [box], trips[box], rows, sources, None)
             for c in range(3):
                 for w, box in enumerate(boxes):
                     near_ref[c * 8 + box : c * 8 + box + 1, :] = lane_sums(total, c, 4 + w)
@@ -351,7 +352,7 @@
 
         @pl.when(sent)
         def _():
-            most = jnp.maximum(trips[boxes[0], 0], trips[boxes[1], 0])
+            most = jnp.maximum(trips[boxes[0]], trips[boxes[1]])
             near_boxes(total, (0, 1), wide_ref, boxes, most, rows, sources, None)
 
     for k in range(8):
@@ -408,7 +409,7 @@
             first_source = (layer - 1) * 2
             for w in range(2):
                 sources = range(first_source, first_source + 6)
-                many = trips[layer * 2 + w, 0]
+                many = trips[layer * 2 + w]
                 near_boxes(total, [w], wide_ref, [plane_box + w], many, rows, sources, late_keep)
             for w in range(2):
                 alive = live[layer * 2 + w : layer * 2 + w + 1] > 0.0
@@ -435,7 +436,7 @@
                             keep[6 + k, at, :] = direct
                     return carry
 
-                lax.fori_loop(0, (trips[layer * 2 + w, 0] + 1) // 2, body, 0)
+                lax.fori_loop(0, (trips[layer * 2 + w] + 1) // 2, body, 0)
 
 
 def fourth_kernel(
@@ -486,7 +487,7 @@
                     total[c, tile_at(tile, (box - 2) * TILE), :] = added([part[c] for part in parts])
             return carry
 
-        lax.fori_loop(0, (trips[box, 0] + 1) // 2, body, 0)
+        lax.fori_loop(0, (trips[box] + 1) // 2, body, 0)
 
     def sweep(boxes, moments):
         for c in range(3):

time: 44.8 us -> 44.3 us (0.989)
  the two profiles are of different devices: /device:TPU:224 before, /device:TPU:97 now
where the time goes in v2:
time: 44.3 us; the launch traced here: 43.8 us
  starting transfers between devices  12.8 us (29%)
  Pallas kernels  12.7 us (29%)
  waiting for transfers between devices  8.92 us (20%)
  blocking collectives  7.23 us (16%)
  local copies, waits for them, and re-layouts  1.36 us (3%)
  between operations  0.76 us (2%)
    all_to_all x1, starting transfers between devices, on_device(): lax.all_to_all(chunk, 'd', 0, 0, axis_index_groups=PLANE_SETS, tiled=True)  6.77 us
    all_to_all x1, waiting for transfers between devices, on_device(): lax.all_to_all(chunk, 'd', 0, 0, axis_index_groups=PLANE_SETS, tiled=True)  6.4 us
    ppermute x1, starting transfers between devices, on_device(): got = lax.ppermute(send, 'd', NEAR_SIDE)  4.13 us
    all_gather x1, blocking collectives, on_device(): lax.all_gather(came, 'd', axis_index_groups=CHIP_SETS, axis=0)  3.84 us
    all_gather x1, blocking collectives, on_device(): own = lax.all_gather(part, 'd', axis_index_groups=CHIP_SETS, axis=0)  3.4 us
    pallas_call x1, Pallas kernels, on_device(): call(second_kernel, [VMEM], [(64, 192), (24, TILE), (4, 8 * TILE, TILE),...  3.01 us
    pallas_call x1, Pallas kernels, on_device(): call(fourth_kernel, [VMEM] * 9, [(3, 2 * TILE), (3, 2 * TILE)], [(3, 16,...  2.92 us
    ppermute x1, waiting for transfers between devices, on_device(): came = lax.ppermute(away, 'd', APART)  2.52 us
  transfers between devices with their start and end apart: 3, of which 2 were waited for; matrix products, arithmetic and copies ran while one was open for 0% of the time, Pallas kernels for 13%

profile of v2, /device:TPU:97, one launch (start us, length us, event | category | flops | bytes accessed | tf_op | source)
XLA Modules:
  0.0 43.8 jit_solution(3306790583414778241)
XLA Ops:
  0.6 2.0 %first.1 = f32[16,40,128]{2,1,0:T(8,128)} custom-call(s32[2]{0:T(128)} %occ_hbm.1, s32[2]{0:T(128)} %count_hbm.1, f32[3,256]{1,0:T(4,128)} %dip_hbm.1, f32[3,256]{1,0:T(4,128)} %perm_hbm.1, f32[3,256]{1,0:T(4,128)} %pos_hbm.1, f32[1,256]{1,0:T(1,128)} %bitcast.14, s32[2,189]{1,0:T(2,128)} %boxes_hbm.1, s32[2,189]{1,0:T(2,128)} %class_hbm.1, f32[2,189]{1,0:T(2,128)} %scale_hbm.1), custom_call_target="tpu_custom_call" | custom-call | flops 1048576 | bytes 1048576 | tf_op jit(solution)/shard_map/first/pallas_call | solution.py:572
  2.6 6.8 %all-to-all-start = ((f32[16,40,128]{2,1,0:T(8,128)}), f32[16,40,128]{2,1,0:T(8,128)S(1)}, u32[]{:S(2)}, u32[]{:S(2)}) async-start(f32[16,40,128]{2,1,0:T(8,128)} %first.1), calls=%async_computation | async-start | bytes 655360 | tf_op jit(solution)/shard_map/all_to_all | solution.py:586
  9.4 0.0 copy-start
  9.5 1.3 %copy-done = f32[8,165,165]{2,0,1:T(8,128)S(1)} copy-done((f32[8,165,165]{2,0,1:T(8,128)S(1)}, f32[8,165,165]{2,0,1:T(8,128)}, u32[]{:S(2)}) %copy-start) | copy-done | bytes 871224
  10.8 0.8 %prepare.1 = (bf16[2048,165]{1,0:T(8,128)(2,1)S(1)}, bf16[2048,165]{1,0:T(8,128)(2,1)S(1)}) custom-call(f32[165,8,165]{2,1,0:T(8,128)S(1)} %bitcast.10), custom_call_target="tpu_custom_call" | custom-call | flops 268435456 | bytes 1048576 | tf_op jit(solution)/shard_map/prepare/pallas_call | solution.py:588
  11.6 6.4 %all-to-all-done.block_ref = f32[16,40,128]{2,1,0:T(8,128)S(1)} async-done(((f32[16,40,128]{2,1,0:T(8,128)}), f32[16,40,128]{2,1,0:T(8,128)S(1)}, u32[]{:S(2)}, u32[]{:S(2)}) %all-to-all-start) | async-done | bytes 327712 | tf_op jit(solution)/shard_map/all_to_all | solution.py:586
  18.0 3.4 %all-gather.own_ref = f32[384,128]{1,0:T(8,128)S(1)} all-gather(f32[192,128]{1,0:T(8,128)S(1)} %pad_maximum_fusion.1), channel_id=2, replica_groups={{0,64},{1,65},{2,66},{3,67},{4,68},{5,69},{6,70},{7,71},{8,72},{9,73},{..., dimensions={0}, use_global_device_ids=true | all-gather | bytes 294912 | tf_op jit(solution)/shard_map/all_gather | solution.py:596
  21.4 1.9 %collective-permute-start = (f32[320,128]{1,0:T(8,128)S(1)}, f32[320,128]{1,0:T(8,128)S(1)}, u32[]{:S(2)}, u32[]{:S(2)}) collective-permute-start(f32[320,128]{1,0:T(8,128)S(1)} %pad_maximum_fusion), channel_id=1, source_target_pairs={{0,4},{1,5},{2,6},{3,7},{4,8},{5,9},{6,10},{7,11},{8,12},{9,13},{1... | collective-permute-start | bytes 491528 | tf_op jit(solution)/shard_map/ppermute | solution.py:599
  23.4 3.0 %second.1 = (f32[64,192]{1,0:T(8,128)S(1)}, f32[24,128]{1,0:T(8,128)S(1)}, f32[4,1024,128]{2,1,0:T(8,128)S(1)}, bf16[1408,128]{1,0:T(8,128)(2,1)S(1)}, bf16[1408...) custom-call(f32[16,40,128]{2,1,0:T(8,128)S(1)} %all-to-all-done.block_ref), custom_call_target="tpu_custom_call" | custom-call | flops 268435456 | bytes 1048576 | tf_op jit(solution)/shard_map/second/pallas_call | solution.py:602
  26.4 2.5 %collective-permute-done = f32[320,128]{1,0:T(8,128)S(1)} collective-permute-done((f32[320,128]{1,0:T(8,128)S(1)}, f32[320,128]{1,0:T(8,128)S(1)}, u32[]{:S(2)}, u32[]{:S(2)}) %collective-permute-start) | collective-permute-done | bytes 163872 | tf_op jit(solution)/shard_map/ppermute | solution.py:599
  28.9 3.8 %all-gather.1.sides_ref = f32[640,128]{1,0:T(8,128)S(1)} all-gather(f32[320,128]{1,0:T(8,128)S(1)} %collective-permute-done), channel_id=3, replica_groups={{0,64},{1,65},{2,66},{3,67},{4,68},{5,69},{6,70},{7,71},{8,72},{9,73},{..., dimensions={0}, use_global_device_ids=true | all-gather | bytes 491520 | tf_op jit(solution)/shard_map/all_gather | solution.py:612
  32.7 2.0 %third.1 = (f32[24,128]{1,0:T(8,128)S(1)}, f32[12,128]{1,0:T(8,128)S(1)}) custom-call(f32[16,40,128]{2,1,0:T(8,128)S(1)} %all-to-all-done.block_ref, f32[384,128]{1,0:T(8,128)S(1)} %all-gather.own_ref, f32[640,128]{1,0:T(8,128)S(1)} %all-gather.1.sides_ref, f32[64,192]{1,0:T(8,128)S(1)} %get-tuple-element.34.sel_ref, ...), custom_call_target="tpu_custom_call" | custom-call | flops 268435456 | bytes 1048576 | tf_op jit(solution)/shard_map/third/pallas_call | solution.py:613
  34.7 4.1 %collective-permute-start.1 = (f32[12,128]{1,0:T(8,128)S(1)}, f32[12,128]{1,0:T(8,128)S(1)}, u32[]{:S(2)}, u32[]{:S(2)}) collective-permute-start(f32[12,128]{1,0:T(8,128)S(1)} %get-tuple-element.41), channel_id=1, source_target_pairs={{0,4},{1,5},{4,8},{5,9},{8,12},{9,13},{12,16},{13,17},{16,20},{17,... | collective-permute-start | bytes 18440 | tf_op jit(solution)/shard_map/ppermute | solution.py:622
  38.8 2.1 %window.1 = (f32[128,128]{1,0:T(8,128)S(1)}, f32[12,256,128]{2,1,0:T(8,128)S(1)}, f32[4,256,128]{2,1,0:T(8,128)S(1)}, f32[12,256,128]{2,1,0:T(8,128)S(1)}, f32[8,128]{1,0:T(8,128)S(1)}) custom-call(f32[16,40,128]{2,1,0:T(8,128)S(1)} %all-to-all-done.block_ref, f32[640,128]{1,0:T(8,128)S(1)} %all-gather.1.sides_ref, ...), custom_call_target="tpu_custom_call" | custom-call | flops 268435456 | bytes 1048576 | tf_op jit(solution)/shard_map/window/pallas_call | solution.py:623
  40.9 0.0 collective-permute-done.1.got_ref
  40.9 2.9 %fourth.1 = (f32[3,256]{1,0:T(4,128)}, f32[3,256]{1,0:T(4,128)}) custom-call(f32[128,128]{1,0:T(8,128)S(1)} %get-tuple-element.28.rows_ref, f32[12,512,128]{2,1,0:T(8,128)S(1)} %get-tuple-element.29.plane_keep, f32[12,256,128]{2,1,0:T(8,128)S(1)} %get-tuple-element.30.late_keep, f32[8,128]{1,0:T(8,128)S(1)} %get-tuple-element.31.late_ref, ...), custom_call_target="tpu_custom_call" | custom-call | flops 268435456 | bytes 1048576 | tf_op jit(solution)/shard_map/fourth/pallas_call | solution.py:632
  (6 shorter events, 0.1 us)
Async XLA Ops:
  2.6 15.3 %all-to-all-start = ((f32[16,40,128]{2,1,0:T(8,128)}), f32[16,40,128]{2,1,0:T(8,128)S(1)}, u32[]{:S(2)}, u32[]{:S(2)}) async-start(f32[16,40,128]{2,1,0:T(8,128)} %first.1), calls=%async_computation | async-start | bytes 655360 | tf_op jit(solution)/shard_map/all_to_all | solution.py:586
  9.4 1.3 %copy-start = (f32[8,165,165]{2,0,1:T(8,128)S(1)}, f32[8,165,165]{2,0,1:T(8,128)}, u32[]{:S(2)}) copy-start(f32[8,165,165]{2,0,1:T(8,128)} %param.19) | copy-start | bytes 2613604
  21.4 7.5 %collective-permute-start = (f32[320,128]{1,0:T(8,128)S(1)}, f32[320,128]{1,0:T(8,128)S(1)}, u32[]{:S(2)}, u32[]{:S(2)}) collective-permute-start(f32[320,128]{1,0:T(8,128)S(1)} %pad_maximum_fusion), channel_id=1, source_target_pairs={{0,4},{1,5},{2,6},{3,7},{4,8},{5,9},{6,10},{7,11},{8,12},{9,13},{1... | collective-permute-start | bytes 491528 | tf_op jit(solution)/shard_map/ppermute | solution.py:599
  34.7 6.2 %collective-permute-start.1 = (f32[12,128]{1,0:T(8,128)S(1)}, f32[12,128]{1,0:T(8,128)S(1)}, u32[]{:S(2)}, u32[]{:S(2)}) collective-permute-start(f32[12,128]{1,0:T(8,128)S(1)} %get-tuple-element.41), channel_id=1, source_target_pairs={{0,4},{1,5},{4,8},{5,9},{8,12},{9,13},{12,16},{13,17},{16,20},{17,... | collective-permute-start | bytes 18440 | tf_op jit(solution)/shard_map/ppermute | solution.py:622

commit v3 on v2

--- a/solution.py
+++ b/solution.py
@@ -136,7 +136,7 @@
         for c in range(3):
             chunk[c * 2 + w : c * 2 + w + 1, :] = moment[c : c + 1, :TILE]
             chunk[6 + w : 7 + w, c * REST : (c + 1) * REST] = moment[c : c + 1, TILE:]
-    whole = chunk[...]
+    whole = chunk[0:CHUNK, :]
     for m in range(PLANE):
         out_ref[m, :, :] = whole
 
@@ -560,6 +560,7 @@
 
 PLANE_SETS, CHIP_SETS, APART, NEAR_SIDE = rounds()
 OWN_ROWS = PLANE * 8 + 64
+MONO_ROWS = (NTERM + 3) * 8
 SIDE_ROWS = 256 + 64
 
 
@@ -573,7 +574,7 @@
         first_kernel,
         [HBM] * 9,
         [(PLANE, CHUNK, TILE)],
-        [(NTERM * 8, TILE), (CHUNK, TILE)]
+        [(MONO_ROWS, TILE), (2 * CHUNK, TILE)]
         + [(3, 2 * TILE)] * 3
         + [(1, 2 * TILE), (2, ILIST), lists, lists, two, two, pltpu.SemaphoreType.DMA((9,))],
         1 << 20,
@@ -603,7 +604,7 @@
         second_kernel,
         [VMEM],
         [(64, 192), (24, TILE), (4, 8 * TILE, TILE), half, half, (12, 4 * TILE, TILE)],
-        [(TILE, TILE), (3, 6 * TILE, TILE), (NTERM * 8, TILE)],
+        [(TILE, TILE), (3, 6 * TILE, TILE), (MONO_ROWS, TILE)],
         1 << 28,
         20,
         "second",
@@ -614,7 +615,7 @@
         third_kernel,
         [VMEM] * 10,
         [(24, TILE), (12, TILE)],
-        [(256, TILE), (48, TILE), (48, TILE), (24, TILE), (TILE, TILE), (3, 2 * TILE, TILE)],
+        [(256, TILE), (64, TILE), (64, TILE), (24, TILE), (TILE, TILE), (3, 2 * TILE, TILE)],
         1 << 28,
         16,
         "third",

time: 44.3 us -> 44.2 us (level)
  starting transfers between devices: 12.8 us -> 13.7 us
  blocking collectives: 7.23 us -> 6.47 us
  Pallas kernels: 12.7 us -> 13.4 us
  waiting for transfers between devices: 8.92 us -> 8.29 us
    ppermute x1, starting transfers between devices: 4.13 us -> 4.97 us  [on_device(): got = lax.ppermute(send, 'd', NEAR_SIDE)]
    all_gather x1, blocking collectives: 3.84 us -> 3.07 us  [on_device(): lax.all_gather(came, 'd', axis_index_groups=CHIP_SETS, axis=0)]
    ppermute x1, waiting for transfers between devices: 2.52 us -> 1.89 us  [on_device(): came = lax.ppermute(away, 'd', APART)]
    pallas_call x1, Pallas kernels: 3.01 us -> 3.64 us  [on_device(): call(second_kernel, [VMEM], [(64, 192), (24, TILE), (4, 8 * TILE, TILE),...]
  transfers between devices with their start and end apart: 3 -> 3, of which waited for: 2 -> 2; matrix products, arithmetic and copies ran while one was open for 0% -> 0% of each run, Pallas kernels for 13% -> 15%
where the time goes in v3:
time: 44.2 us; the launch traced here: 44 us
  starting transfers between devices  13.7 us (31%)
  Pallas kernels  13.4 us (30%)
  waiting for transfers between devices  8.29 us (19%)
  blocking collectives  6.47 us (15%)
  local copies, waits for them, and re-layouts  1.36 us (3%)
  between operations  0.76 us (2%)
    all_to_all x1, starting transfers between devices, on_device(): lax.all_to_all(chunk, 'd', 0, 0, axis_index_groups=PLANE_SETS, tiled=True)  6.77 us
    all_to_all x1, waiting for transfers between devices, on_device(): lax.all_to_all(chunk, 'd', 0, 0, axis_index_groups=PLANE_SETS, tiled=True)  6.4 us
    ppermute x1, starting transfers between devices, on_device(): got = lax.ppermute(send, 'd', NEAR_SIDE)  4.97 us
    pallas_call x1, Pallas kernels, on_device(): call(second_kernel, [VMEM], [(64, 192), (24, TILE), (4, 8 * TILE, TILE),...  3.64 us
    all_gather x1, blocking collectives, on_device(): own = lax.all_gather(part, 'd', axis_index_groups=CHIP_SETS, axis=0)  3.4 us
    pallas_call x1, Pallas kernels, on_device(): call(fourth_kernel, [VMEM] * 9, [(3, 2 * TILE), (3, 2 * TILE)], [(3, 16,...  3.12 us
    all_gather x1, blocking collectives, on_device(): lax.all_gather(came, 'd', axis_index_groups=CHIP_SETS, axis=0)  3.07 us
    pallas_call x1, Pallas kernels, on_device(): call(window_kernel, [VMEM] * 3, [(TILE, TILE), (12, 2 * TILE, TILE), (4,...  2.06 us
  transfers between devices with their start and end apart: 3, of which 2 were waited for; matrix products, arithmetic and copies ran while one was open for 0% of the time, Pallas kernels for 15%

profile of v3, /device:TPU:97, one launch (start us, length us, event | category | flops | bytes accessed | tf_op | source)
XLA Modules:
  0.0 44.0 jit_solution(8190762743431599431)
XLA Ops:
  0.6 2.0 %first.1 = f32[16,40,128]{2,1,0:T(8,128)} custom-call(s32[2]{0:T(128)} %occ_hbm.1, s32[2]{0:T(128)} %count_hbm.1, f32[3,256]{1,0:T(4,128)} %dip_hbm.1, f32[3,256]{1,0:T(4,128)} %perm_hbm.1, f32[3,256]{1,0:T(4,128)} %pos_hbm.1, f32[1,256]{1,0:T(1,128)} %bitcast.14, s32[2,189]{1,0:T(2,128)} %boxes_hbm.1, s32[2,189]{1,0:T(2,128)} %class_hbm.1, f32[2,189]{1,0:T(2,128)} %scale_hbm.1), custom_call_target="tpu_custom_call" | custom-call | flops 1048576 | bytes 1048576 | tf_op jit(solution)/shard_map/first/pallas_call | solution.py:573
  2.6 6.8 %all-to-all-start = ((f32[16,40,128]{2,1,0:T(8,128)}), f32[16,40,128]{2,1,0:T(8,128)S(1)}, u32[]{:S(2)}, u32[]{:S(2)}) async-start(f32[16,40,128]{2,1,0:T(8,128)} %first.1), calls=%async_computation | async-start | bytes 655360 | tf_op jit(solution)/shard_map/all_to_all | solution.py:587
  9.4 0.0 copy-start
  9.5 1.3 %copy-done = f32[8,165,165]{2,0,1:T(8,128)S(1)} copy-done((f32[8,165,165]{2,0,1:T(8,128)S(1)}, f32[8,165,165]{2,0,1:T(8,128)}, u32[]{:S(2)}) %copy-start) | copy-done | bytes 871224
  10.8 0.8 %prepare.1 = (bf16[2048,165]{1,0:T(8,128)(2,1)S(1)}, bf16[2048,165]{1,0:T(8,128)(2,1)S(1)}) custom-call(f32[165,8,165]{2,1,0:T(8,128)S(1)} %bitcast.10), custom_call_target="tpu_custom_call" | custom-call | flops 268435456 | bytes 1048576 | tf_op jit(solution)/shard_map/prepare/pallas_call | solution.py:589
  11.6 6.4 %all-to-all-done.block_ref = f32[16,40,128]{2,1,0:T(8,128)S(1)} async-done(((f32[16,40,128]{2,1,0:T(8,128)}), f32[16,40,128]{2,1,0:T(8,128)S(1)}, u32[]{:S(2)}, u32[]{:S(2)}) %all-to-all-start) | async-done | bytes 327712 | tf_op jit(solution)/shard_map/all_to_all | solution.py:587
  18.0 3.4 %all-gather.own_ref = f32[384,128]{1,0:T(8,128)S(1)} all-gather(f32[192,128]{1,0:T(8,128)S(1)} %pad_maximum_fusion.1), channel_id=2, replica_groups={{0,64},{1,65},{2,66},{3,67},{4,68},{5,69},{6,70},{7,71},{8,72},{9,73},{..., dimensions={0}, use_global_device_ids=true | all-gather | bytes 294912 | tf_op jit(solution)/shard_map/all_gather | solution.py:597
  21.4 1.9 %collective-permute-start = (f32[320,128]{1,0:T(8,128)S(1)}, f32[320,128]{1,0:T(8,128)S(1)}, u32[]{:S(2)}, u32[]{:S(2)}) collective-permute-start(f32[320,128]{1,0:T(8,128)S(1)} %pad_maximum_fusion), channel_id=1, source_target_pairs={{0,4},{1,5},{2,6},{3,7},{4,8},{5,9},{6,10},{7,11},{8,12},{9,13},{1... | collective-permute-start | bytes 491528 | tf_op jit(solution)/shard_map/ppermute | solution.py:600
  23.4 3.6 %second.1 = (f32[64,192]{1,0:T(8,128)S(1)}, f32[24,128]{1,0:T(8,128)S(1)}, f32[4,1024,128]{2,1,0:T(8,128)S(1)}, bf16[1408,128]{1,0:T(8,128)(2,1)S(1)}, bf16[1408...) custom-call(f32[16,40,128]{2,1,0:T(8,128)S(1)} %all-to-all-done.block_ref), custom_call_target="tpu_custom_call" | custom-call | flops 268435456 | bytes 1048576 | tf_op jit(solution)/shard_map/second/pallas_call | solution.py:603
  27.0 1.9 %collective-permute-done = f32[320,128]{1,0:T(8,128)S(1)} collective-permute-done((f32[320,128]{1,0:T(8,128)S(1)}, f32[320,128]{1,0:T(8,128)S(1)}, u32[]{:S(2)}, u32[]{:S(2)}) %collective-permute-start) | collective-permute-done | bytes 163872 | tf_op jit(solution)/shard_map/ppermute | solution.py:600
  28.9 3.1 %all-gather.1.sides_ref = f32[640,128]{1,0:T(8,128)S(1)} all-gather(f32[320,128]{1,0:T(8,128)S(1)} %collective-permute-done), channel_id=3, replica_groups={{0,64},{1,65},{2,66},{3,67},{4,68},{5,69},{6,70},{7,71},{8,72},{9,73},{..., dimensions={0}, use_global_device_ids=true | all-gather | bytes 491520 | tf_op jit(solution)/shard_map/all_gather | solution.py:613
  32.0 1.8 %third.1 = (f32[24,128]{1,0:T(8,128)S(1)}, f32[12,128]{1,0:T(8,128)S(1)}) custom-call(f32[16,40,128]{2,1,0:T(8,128)S(1)} %all-to-all-done.block_ref, f32[384,128]{1,0:T(8,128)S(1)} %all-gather.own_ref, f32[640,128]{1,0:T(8,128)S(1)} %all-gather.1.sides_ref, f32[64,192]{1,0:T(8,128)S(1)} %get-tuple-element.34.sel_ref, ...), custom_call_target="tpu_custom_call" | custom-call | flops 268435456 | bytes 1048576 | tf_op jit(solution)/shard_map/third/pallas_call | solution.py:614
  33.8 5.0 %collective-permute-start.1 = (f32[12,128]{1,0:T(8,128)S(1)}, f32[12,128]{1,0:T(8,128)S(1)}, u32[]{:S(2)}, u32[]{:S(2)}) collective-permute-start(f32[12,128]{1,0:T(8,128)S(1)} %get-tuple-element.41), channel_id=1, source_target_pairs={{0,4},{1,5},{4,8},{5,9},{8,12},{9,13},{12,16},{13,17},{16,20},{17,... | collective-permute-start | bytes 18440 | tf_op jit(solution)/shard_map/ppermute | solution.py:623
  38.8 2.1 %window.1 = (f32[128,128]{1,0:T(8,128)S(1)}, f32[12,256,128]{2,1,0:T(8,128)S(1)}, f32[4,256,128]{2,1,0:T(8,128)S(1)}, f32[12,256,128]{2,1,0:T(8,128)S(1)}, f32[8,128]{1,0:T(8,128)S(1)}) custom-call(f32[16,40,128]{2,1,0:T(8,128)S(1)} %all-to-all-done.block_ref, f32[640,128]{1,0:T(8,128)S(1)} %all-gather.1.sides_ref, ...), custom_call_target="tpu_custom_call" | custom-call | flops 268435456 | bytes 1048576 | tf_op jit(solution)/shard_map/window/pallas_call | solution.py:624
  40.8 0.0 collective-permute-done.1.got_ref
  40.8 3.1 %fourth.1 = (f32[3,256]{1,0:T(4,128)}, f32[3,256]{1,0:T(4,128)}) custom-call(f32[128,128]{1,0:T(8,128)S(1)} %get-tuple-element.28.rows_ref, f32[12,512,128]{2,1,0:T(8,128)S(1)} %get-tuple-element.29.plane_keep, f32[12,256,128]{2,1,0:T(8,128)S(1)} %get-tuple-element.30.late_keep, f32[8,128]{1,0:T(8,128)S(1)} %get-tuple-element.31.late_ref, ...), custom_call_target="tpu_custom_call" | custom-call | flops 268435456 | bytes 1048576 | tf_op jit(solution)/shard_map/fourth/pallas_call | solution.py:633
  (6 shorter events, 0.1 us)
Async XLA Ops:
  2.6 15.3 %all-to-all-start = ((f32[16,40,128]{2,1,0:T(8,128)}), f32[16,40,128]{2,1,0:T(8,128)S(1)}, u32[]{:S(2)}, u32[]{:S(2)}) async-start(f32[16,40,128]{2,1,0:T(8,128)} %first.1), calls=%async_computation | async-start | bytes 655360 | tf_op jit(solution)/shard_map/all_to_all | solution.py:587
  9.4 1.3 %copy-start = (f32[8,165,165]{2,0,1:T(8,128)S(1)}, f32[8,165,165]{2,0,1:T(8,128)}, u32[]{:S(2)}) copy-start(f32[8,165,165]{2,0,1:T(8,128)} %param.19) | copy-start | bytes 2613604
  21.4 7.5 %collective-permute-start = (f32[320,128]{1,0:T(8,128)S(1)}, f32[320,128]{1,0:T(8,128)S(1)}, u32[]{:S(2)}, u32[]{:S(2)}) collective-permute-start(f32[320,128]{1,0:T(8,128)S(1)} %pad_maximum_fusion), channel_id=1, source_target_pairs={{0,4},{1,5},{2,6},{3,7},{4,8},{5,9},{6,10},{7,11},{8,12},{9,13},{1... | collective-permute-start | bytes 491528 | tf_op jit(solution)/shard_map/ppermute | solution.py:600
  33.8 7.1 %collective-permute-start.1 = (f32[12,128]{1,0:T(8,128)S(1)}, f32[12,128]{1,0:T(8,128)S(1)}, u32[]{:S(2)}, u32[]{:S(2)}) collective-permute-start(f32[12,128]{1,0:T(8,128)S(1)} %get-tuple-element.41), channel_id=1, source_target_pairs={{0,4},{1,5},{4,8},{5,9},{8,12},{9,13},{12,16},{13,17},{16,20},{17,... | collective-permute-start | bytes 18440 | tf_op jit(solution)/shard_map/ppermute | solution.py:623
